TPU v7x, 32 devices: a whole 2x2x4 slice. The times are simulated.
32 devices in a mesh: ctx: 16 (over z, y, core), head: 2 (over x).
Axes of the slice: x: 2, y: 2, z: 4, core: 2. Of those that a mesh axis runs over, the one named last changes fastest.
Arguments:
- queries: bfloat16 [12288, 1024], P(('ctx', 'head')), may hold values from -64 to 64
- keys: bfloat16 [12288, 256], P(('ctx', 'head')), may hold values from -6 to 6
- values: bfloat16 [12288, 256], P(('ctx', 'head')), may hold values from -6 to 6
- out_grad: bfloat16 [12288, 1024], P(('ctx', 'head')), may hold values from -6 to 6
- rand_blocks: int32 [96, 3], replicated, may hold values from 0 to 95, as said below
- rand_count: int32 [96], replicated, may hold values from 1 to 3
Outputs:
- query_grad: bfloat16 [12288, 1024], P('ctx', 'head')
- key_grad: bfloat16 [12288, 256], P('ctx', 'head')
- value_grad: bfloat16 [12288, 256], P('ctx', 'head')
Inputs may be any that keep to these rules, and one draw needn't show every extreme that they name: Entry rand_blocks[b, r] names a block of a ctx shard (a range of 6 blocks) that is neither b's own shard nor either neighbour of it, counted modulo 16. The 18 entries of one shard's query blocks name blocks of one other shard at most 2 times, exactly 2 times for some shard.
All inputs are finite; a program needn't handle non-finite values.
Results may differ from a plain program's by a relative error of at most 0.0087.
Values may be sent and summed in bfloat16 or wider, within the bound.
A program may use at most 64 MiB of HBM per device.

v0:
```python
import math
import jax
import jax.numpy as jnp
from jax import lax
from jax.sharding import PartitionSpec as P

BLOCK = 128
HD = 128
GROUP = 4
G = 2
RAND = 3
QB_DEV = 6
NKB = 8


def broadcast(array, axis, root):
    mine = lax.axis_index(axis) == root
    return lax.psum(jnp.where(mine, array, jnp.zeros_like(array)), axis)


def attend(unused, inputs):
    query_tile, grad_tile, pair_tile, mask_row = inputs
    factor = 1.0 / math.sqrt(HD)
    key_tile = pair_tile[:, :, :HD].reshape(NKB * BLOCK, HD)
    value_tile = pair_tile[:, :, HD:].reshape(NKB * BLOCK, HD)
    key_mask = jnp.repeat(mask_row, BLOCK)
    scores = (
        jnp.einsum("tgh,kh->tgk", query_tile, key_tile, preferred_element_type=jnp.float32) * factor
    )
    scores = jnp.where(key_mask[None, None, :], scores, -jnp.inf)
    row_max = jnp.max(scores, axis=-1, keepdims=True)
    raw_weights = jnp.exp(scores - row_max)
    weights = raw_weights / jnp.sum(raw_weights, axis=-1, keepdims=True)
    weights_low = weights.astype(jnp.bfloat16)
    output = jnp.einsum("tgk,kh->tgh", weights_low, value_tile, preferred_element_type=jnp.float32)
    row_dot = jnp.sum(grad_tile.astype(jnp.float32) * output, axis=-1, keepdims=True)
    dprobs = jnp.einsum("tgh,kh->tgk", grad_tile, value_tile, preferred_element_type=jnp.float32)
    dscores = (weights * (dprobs - row_dot)).astype(jnp.bfloat16)
    dquery = (
        jnp.einsum("tgk,kh->tgh", dscores, key_tile, preferred_element_type=jnp.float32) * factor
    ).astype(jnp.bfloat16)
    key_part = (
        jnp.einsum("tgk,tgh->kh", dscores, query_tile, preferred_element_type=jnp.float32) * factor
    )
    value_part = jnp.einsum(
        "tgk,tgh->kh", weights_low, grad_tile, preferred_element_type=jnp.float32
    )
    pair_grad = jnp.concatenate(
        [key_part.reshape(NKB, BLOCK, HD), value_part.reshape(NKB, BLOCK, HD)], axis=-1
    )
    return (unused, (dquery, pair_grad))


def body(queries, keys, values, out_grad, rand_blocks, rand_count):
    head_queries, head_keys, head_values, head_grads = (
        lax.all_to_all(queries, "head", split_axis=1, concat_axis=0, tiled=True),
        lax.all_to_all(keys, "head", split_axis=1, concat_axis=0, tiled=True),
        lax.all_to_all(values, "head", split_axis=1, concat_axis=0, tiled=True),
        lax.all_to_all(out_grad, "head", split_axis=1, concat_axis=0, tiled=True),
    )
    shards = lax.axis_size("ctx")
    myself = lax.axis_index("ctx")
    per_dev = QB_DEV
    entries = per_dev * RAND
    owners_used = min(entries, shards - 3)
    capacity = (entries + owners_used - 1) // owners_used
    total_blocks = per_dev * shards
    far_slots = shards * capacity
    local_pairs = jnp.concatenate([head_keys, head_values], axis=1).reshape(per_dev, BLOCK, 2 * HD)
    global_pairs = broadcast(local_pairs[:G], "ctx", 0)
    flat_blocks = rand_blocks.reshape(shards, entries)
    owners = flat_blocks // per_dev
    offsets = flat_blocks % per_dev
    positions = jnp.arange(entries, dtype=jnp.int32)
    earlier = positions[None, :] < positions[:, None]
    same_owner = owners[:, :, None] == owners[:, None, :]
    slot_ranks = jnp.sum(same_owner & earlier[None], axis=2)
    slot_range = jnp.arange(capacity, dtype=jnp.int32)
    send_hits = (
        (owners == myself)[:, None, :] & (slot_ranks[:, None, :] == slot_range[None, :, None])
    ).astype(jnp.float32)
    offset_hot = (
        offsets[:, :, None] == jnp.arange(per_dev, dtype=jnp.int32)[None, None, :]
    ).astype(jnp.float32)
    send_table = jnp.einsum("dme,deq->dmq", send_hits, offset_hot)
    edge_base = per_dev + far_slots
    targets = jnp.arange(shards, dtype=jnp.int32)[:, None, None]
    first_slot = (slot_range == 0)[None, :, None]
    block_range = jnp.arange(per_dev, dtype=jnp.int32)[None, None, :]
    right_send = (targets == (myself + 1) % shards) & first_slot & (block_range == per_dev - 1)
    left_send = (targets == (myself - 1 + shards) % shards) & first_slot & (block_range == 0)
    send_table = send_table + right_send.astype(jnp.float32) + left_send.astype(jnp.float32)
    edge_pairs = jnp.zeros((0, BLOCK, 2 * HD), jnp.bfloat16)
    left_far = per_dev + (myself - 1 + shards) % shards * capacity
    right_far = per_dev + (myself + 1) % shards * capacity
    outgoing = jnp.einsum(
        "dmq,qtc->dmtc",
        send_table.astype(jnp.bfloat16),
        local_pairs,
        preferred_element_type=jnp.float32,
    ).astype(jnp.bfloat16)
    far_pairs = lax.all_to_all(outgoing, "ctx", split_axis=0, concat_axis=0, tiled=True)
    block_pool = jnp.concatenate(
        [local_pairs, far_pairs.reshape(far_slots, BLOCK, 2 * HD), edge_pairs, global_pairs], axis=0
    )
    local_index = jnp.arange(per_dev, dtype=jnp.int32)
    seq_block = myself * per_dev + local_index
    left_index = jnp.where(local_index > 0, local_index - 1, left_far)
    right_index = jnp.where(local_index < per_dev - 1, local_index + 1, right_far)
    global_index = jnp.broadcast_to(
        edge_base + jnp.arange(G, dtype=jnp.int32)[None, :], (per_dev, G)
    )
    my_owners = lax.dynamic_index_in_dim(owners, myself, 0, keepdims=False)
    my_ranks = lax.dynamic_index_in_dim(slot_ranks, myself, 0, keepdims=False)
    random_index = (per_dev + my_owners * capacity + my_ranks).reshape(per_dev, RAND)
    key_table = jnp.concatenate(
        [jnp.stack([left_index, local_index, right_index], axis=1), global_index, random_index],
        axis=1,
    )
    my_counts = lax.dynamic_slice_in_dim(rand_count, myself * per_dev, per_dev)
    key_valid = jnp.concatenate(
        [
            jnp.stack([seq_block > 0, seq_block >= 0, seq_block < total_blocks - 1], axis=1),
            jnp.ones((per_dev, G), bool),
            jnp.arange(RAND, dtype=jnp.int32)[None, :] < my_counts[:, None],
        ],
        axis=1,
    )
    remote = (key_table >= per_dev) & (key_table < edge_base)
    gathered = block_pool[key_table]
    query_tiles = head_queries.reshape(per_dev, BLOCK, GROUP, HD)
    grad_tiles = head_grads.reshape(per_dev, BLOCK, GROUP, HD)
    unused, (dq_tiles, pair_grads) = lax.scan(
        attend, jnp.zeros((), jnp.float32), (query_tiles, grad_tiles, gathered, key_valid)
    )
    lowered = lax.optimization_barrier(pair_grads.astype(jnp.bfloat16)).astype(jnp.float32)
    pair_grads = jnp.where(remote[:, :, None, None], lowered, pair_grads)
    pool_size = edge_base + G
    pool_hot = (
        key_table[:, :, None] == jnp.arange(pool_size, dtype=jnp.int32)[None, None, :]
    ).astype(jnp.float32)
    pool_grads = jnp.einsum("jnp,jntc->ptc", pool_hot, pair_grads, precision=lax.Precision.HIGHEST)
    local_grads = pool_grads[:per_dev]
    outgoing_grads = (
        pool_grads[per_dev:edge_base].reshape(shards, capacity, BLOCK, 2 * HD).astype(jnp.bfloat16)
    )
    returned = lax.all_to_all(outgoing_grads, "ctx", split_axis=0, concat_axis=0, tiled=True)
    local_grads = local_grads + jnp.einsum(
        "dmq,dmtc->qtc", send_table, returned.astype(jnp.float32), precision=lax.Precision.HIGHEST
    )
    global_total = lax.psum(pool_grads[edge_base:], "ctx")
    local_grads = local_grads.at[:G].add(
        jnp.where(myself == 0, global_total, jnp.zeros_like(global_total))
    )
    query_grad = dq_tiles.reshape(per_dev * BLOCK, GROUP * HD)
    key_grad = local_grads[:, :, :HD].reshape(per_dev * BLOCK, HD).astype(jnp.bfloat16)
    value_grad = local_grads[:, :, HD:].reshape(per_dev * BLOCK, HD).astype(jnp.bfloat16)
    return (query_grad, key_grad, value_grad)


def solution(mesh):
    placed = (
        P(("ctx", "head"), None),
        P(("ctx", "head"), None),
        P(("ctx", "head"), None),
        P(("ctx", "head"), None),
        P(),
        P(),
    )
    return jax.shard_map(
        body,
        mesh=mesh,
        in_specs=placed,
        out_specs=(P("ctx", "head"), P("ctx", "head"), P("ctx", "head")),
        check_vma=False,
    )
```

profile of v0, /device:TPU:0, one launch (start us, length us, event | category | flops | bytes accessed | tf_op | source)
XLA Modules:
  0.0 388.8 jit_solution(16370104756201506846)
XLA Ops:
  7.2 1.8 copy.167
  9.0 4.2 %all-to-all-start.2 = ((bf16[384,2,128]{0,2,1:T(8,128)(2,1)}), bf16[384,2,128]{0,2,1:T(8,128)(2,1)S(1)}, u32[]{:S(2)}, u32[]{:S(2)}) async-start(bf16[384,2,128]{0,2,1:T(8,128)(2,1)} %bitcast.24), calls=%async_computation.2 | async-start | bytes 393216 | tf_op jit(solution)/shard_map/all_to_all | solution.py:58
  14.6 2.1 copy.243
  19.0 3.5 all-to-all-start.1
  22.4 5.1 %all-to-all-done.1 = bf16[384,2,128]{0,2,1:T(8,128)(2,1)S(1)} async-done(((bf16[384,2,128]{0,2,1:T(8,128)(2,1)}), bf16[384,2,128]{0,2,1:T(8,128)(2,1)S(1)}, u32[]{:S(2)}, u32[]{:S(2)}) %all-to-all-start.1) | async-done | bytes 196640 | tf_op jit(solution)/shard_map/all_to_all | solution.py:57
  27.6 3.5 all-to-all-start
  32.7 8.9 %all-to-all-done = bf16[384,2,512]{2,0,1:T(8,128)(2,1)S(1)} async-done(((bf16[384,2,512]{2,0,1:T(8,128)(2,1)}), bf16[384,2,512]{2,0,1:T(8,128)(2,1)S(1)}, u32[]{:S(2)}, u32[]{:S(2)}) %all-to-all-start) | async-done | bytes 786464 | tf_op jit(solution)/shard_map/all_to_all | solution.py:56
  41.6 3.5 all-to-all-start.4
  46.2 2.1 copy.177
  48.3 6.4 %all-to-all-done.4 = bf16[384,2,512]{2,0,1:T(8,128)(2,1)S(1)} async-done(((bf16[384,2,512]{2,0,1:T(8,128)(2,1)}), bf16[384,2,512]{2,0,1:T(8,128)(2,1)S(1)}, u32[]{:S(2)}, u32[]{:S(2)}) %all-to-all-start.4) | async-done | bytes 786464 | tf_op jit(solution)/shard_map/all_to_all | solution.py:59
  55.7 5.1 %all-to-all-start.3 = ((bf16[16,2,128,256]{3,2,1,0:T(8,128)(2,1)}), bf16[16,2,128,256]{3,2,1,0:T(8,128)(2,1)S(1)}, u32[]{:S(2)}, u32[]{:S(2)}) async-start(bf16[16,2,128,256]{3,2,1,0:T(8,128)(2,1)} %copy.177), calls=%async_computation.3 | async-start | bytes 4194304 | tf_op jit(solution)/shard_map/all_to_all | solution.py:102
  62.9 1.5 fusion.29
  65.3 1.0 reshape.535
  66.4 1.7 reshape.537
  68.1 104.0 %all-reduce.3.cloned.1.call-done = bf16[2,128,256]{2,1,0:T(8,128)(2,1)} async-done(((bf16[2,128,256]{2,1,0:T(8,128)(2,1)}), bf16[2,128,256]{2,1,0:T(8,128)(2,1)}) %all-reduce.3.cloned.1.call-update) | async-done | bytes 131088 | tf_op jit(solution)/shard_map/psum | solution.py:18
  172.1 1.4 copy-done.2
  173.5 2.0 pad_maximum_fusion
  175.5 2.6 gather_fusion
  178.1 49.3 %while.13 = (s32[]{:T(128)}, bf16[6,128,4,128]{3,2,1,0:T(4,128)(2,1)}, f32[6,8,128,256]{2,3,1,0:T(8,128)}, pred[6,8]{1,0:T(8,128)(4,1)S(1)}, bf16[6,128,4,128]{3...) while((s32[]{:T(128)}, ...), condition=%wide.region_6.7_spmd, body=%wide.region_2.6_spmd.sunk | while | flops 814414336 | bytes 22569096 | solution.py:133
  178.1 1.1 dynamic-slice_bitcast_fusion.4
  179.3 1.0 constant_dynamic-slice_fusion.5
  185.3 1.1 fusion.107
  186.3 1.1 dynamic-slice_bitcast_fusion.4
  193.5 1.1 fusion.107
  194.5 1.1 dynamic-slice_bitcast_fusion.4
  201.7 1.1 fusion.107
  202.7 1.1 dynamic-slice_bitcast_fusion.4
  209.9 1.1 fusion.107
  211.0 1.1 dynamic-slice_bitcast_fusion.4
  218.1 1.1 fusion.107
  219.2 1.1 dynamic-slice_bitcast_fusion.4
  226.3 1.1 fusion.107
  227.4 3.4 convert_element_type.57
  230.8 1.1 copy-done
  232.0 3.9 convert_select_fusion
  235.9 6.7 %copy.188 = f32[6,8,128,256]{3,1,0,2:T(8,128)} copy(f32[6,8,128,256]{2,3,1,0:T(8,128)} %convert_select_fusion) | data formatting | bytes 12582912 | tf_op jit(solution)/shard_map/jit(_where)/select_n | solution.py:137
  242.6 5.0 %convolution_bitcast_fusion.2 = f32[40,128,256]{2,0,1:T(8,128)S(1)} fusion(f32[6,8,128,256]{3,1,0,2:T(8,128)} %copy.188, s32[6,8]{1,0:T(8,128)S(1)} %concatenate.68), kind=kOutput, calls=%fused_computation.38 | convolution fusion | flops 754976640 | bytes 11534528 | tf_op jit(solution)/shard_map/jnp,jntc->ptc/dot_general | solution.py:142
  247.6 2.3 copy-done.1
  249.9 2.0 slice.74
  251.9 2.7 convert_element_type.59
  254.7 3.4 copy.189
  258.1 6.7 %all-to-all-start.5 = ((bf16[16,2,128,256]{3,1,2,0:T(2,128)(2,1)}), bf16[16,2,128,256]{3,1,2,0:T(2,128)(2,1)S(1)}, u32[]{:S(2)}, u32[]{:S(2)}) async-start(bf16[16,2,128,256]{3,1,2,0:T(2,128)(2,1)} %copy.189), calls=%async_computation.5 | async-start | bytes 4194304 | tf_op jit(solution)/shard_map/all_to_all | solution.py:147
  264.8 2.0 slice.66
  266.9 1.0 copy.241
  267.9 39.2 %all-to-all-done.5 = bf16[16,2,128,256]{3,1,2,0:T(2,128)(2,1)S(1)} async-done(((bf16[16,2,128,256]{3,1,2,0:T(2,128)(2,1)}), bf16[16,2,128,256]{3,1,2,0:T(2,128)(2,1)S(1)}, u32[]{:S(2)}, u32[]{:S(2)}) %all-to-all-start.5) | async-done | bytes 2097184 | tf_op jit(solution)/shard_map/all_to_all | solution.py:147
  307.1 3.2 fusion.24
  310.4 68.8 %all-reduce.5.cloned.1.call-done = f32[2,128,256]{2,0,1:T(2,128)} async-done(((f32[2,128,256]{2,0,1:T(2,128)}), f32[2,128,256]{2,0,1:T(2,128)}) %all-reduce.5.cloned.1.call-update) | async-done | bytes 262160 | tf_op jit(solution)/shard_map/psum | solution.py:151
  379.1 1.2 fusion.28
  (157 shorter events, 46.8 us)
Async XLA Ops:
  7.2 9.6 %copy-start.8 = (bf16[384,256]{1,0:T(8,128)(2,1)S(1)}, bf16[384,256]{1,0:T(8,128)(2,1)}, u32[]{:S(2)}) copy-start(bf16[384,256]{1,0:T(8,128)(2,1)} %param.11) | copy-start | bytes 589828
  9.0 10.0 %all-to-all-start.2 = ((bf16[384,2,128]{0,2,1:T(8,128)(2,1)}), bf16[384,2,128]{0,2,1:T(8,128)(2,1)S(1)}, u32[]{:S(2)}, u32[]{:S(2)}) async-start(bf16[384,2,128]{0,2,1:T(8,128)(2,1)} %bitcast.24), calls=%async_computation.2 | async-start | bytes 393216 | tf_op jit(solution)/shard_map/all_to_all | solution.py:58
  14.6 16.7 %copy-start.6 = (bf16[384,1024]{1,0:T(8,128)(2,1)S(1)}, bf16[384,1024]{1,0:T(8,128)(2,1)}, u32[]{:S(2)}) copy-start(bf16[384,1024]{1,0:T(8,128)(2,1)} %param.13) | copy-start | bytes 2359300
  19.0 8.6 %all-to-all-start.1 = ((bf16[384,2,128]{0,2,1:T(8,128)(2,1)}), bf16[384,2,128]{0,2,1:T(8,128)(2,1)S(1)}, u32[]{:S(2)}, u32[]{:S(2)}) async-start(bf16[384,2,128]{0,2,1:T(8,128)(2,1)} %bitcast.21), calls=%async_computation.1 | async-start | bytes 393216 | tf_op jit(solution)/shard_map/all_to_all | solution.py:57
  27.6 14.0 %all-to-all-start = ((bf16[384,2,512]{2,0,1:T(8,128)(2,1)}), bf16[384,2,512]{2,0,1:T(8,128)(2,1)S(1)}, u32[]{:S(2)}, u32[]{:S(2)}) async-start(bf16[384,2,512]{2,0,1:T(8,128)(2,1)} %bitcast.127), calls=%async_computation | async-start | bytes 1572864 | tf_op jit(solution)/shard_map/all_to_all | solution.py:56
  32.4 13.8 %copy-start.4 = (bf16[2,384,128]{2,1,0:T(8,128)(2,1)}, bf16[2,384,128]{2,1,0:T(8,128)(2,1)S(1)}, u32[]{:S(2)}) copy-start(bf16[2,384,128]{2,1,0:T(8,128)(2,1)S(1)} %copy.168) | copy-start | bytes 589828
  32.6 9.0 %copy-start.5 = (bf16[2,384,128]{2,1,0:T(8,128)(2,1)}, bf16[2,384,128]{2,1,0:T(8,128)(2,1)S(1)}, u32[]{:S(2)}) copy-start(bf16[2,384,128]{2,1,0:T(8,128)(2,1)S(1)} %copy.166) | copy-start | bytes 589828
  41.6 13.1 %all-to-all-start.4 = ((bf16[384,2,512]{2,0,1:T(8,128)(2,1)}), bf16[384,2,512]{2,0,1:T(8,128)(2,1)S(1)}, u32[]{:S(2)}, u32[]{:S(2)}) async-start(bf16[384,2,512]{2,0,1:T(8,128)(2,1)} %bitcast.126), calls=%async_computation.4 | async-start | bytes 1572864 | tf_op jit(solution)/shard_map/all_to_all | solution.py:59
  48.3 14.2 %copy-start.9 = (s32[96]{0:T(128)S(1)}, s32[96]{0:T(128)}, u32[]{:S(2)}) copy-start(s32[96]{0:T(128)} %param.15) | copy-start | bytes 1156
  54.7 1.0 copy-start.3
  55.7 116.4 %all-to-all-start.3 = ((bf16[16,2,128,256]{3,2,1,0:T(8,128)(2,1)}), bf16[16,2,128,256]{3,2,1,0:T(8,128)(2,1)S(1)}, u32[]{:S(2)}, u32[]{:S(2)}) async-start(bf16[16,2,128,256]{3,2,1,0:T(8,128)(2,1)} %copy.177), calls=%async_computation.3 | async-start | bytes 4194304 | tf_op jit(solution)/shard_map/all_to_all | solution.py:102
  60.8 111.4 %all-reduce.3.cloned.1.call-start = ((), (), s32[]{:S(2)}) async-start(), calls=%async_computation.6 | async-start | bytes 262144 | tf_op jit(solution)/shard_map/psum | solution.py:18
  172.1 1.4 copy-start.2
  227.4 4.6 %copy-start = (f32[6,8,128,256]{2,3,1,0:T(8,128)S(1)}, f32[6,8,128,256]{2,3,1,0:T(8,128)}, u32[]{:S(2)}) copy-start(f32[6,8,128,256]{2,3,1,0:T(8,128)} %get-tuple-element.54) | copy-start | bytes 18874372
  247.6 2.3 copy-start.1
  258.1 8.8 %copy-start.7 = (bf16[6,128,4,128]{3,2,1,0:T(4,128)(2,1)S(1)}, bf16[6,128,4,128]{3,2,1,0:T(4,128)(2,1)}, u32[]{:S(2)}) copy-start(bf16[6,128,4,128]{3,2,1,0:T(4,128)(2,1)} %get-tuple-element.53) | copy-start | bytes 2359300
  258.1 49.1 %all-to-all-start.5 = ((bf16[16,2,128,256]{3,1,2,0:T(2,128)(2,1)}), bf16[16,2,128,256]{3,1,2,0:T(2,128)(2,1)S(1)}, u32[]{:S(2)}, u32[]{:S(2)}) async-start(bf16[16,2,128,256]{3,1,2,0:T(2,128)(2,1)} %copy.189), calls=%async_computation.5 | async-start | bytes 4194304 | tf_op jit(solution)/shard_map/all_to_all | solution.py:147
  264.8 114.4 %all-reduce.5.cloned.1.call-start = ((), (), s32[]{:S(2)}) async-start(), calls=%async_computation.7 | async-start | bytes 524288 | tf_op jit(solution)/shard_map/psum | solution.py:151
Sparse Core Ops, SparseCore 0:
  65.1 107.0 all-reduce.2
  269.0 110.0 all-reduce.4
where the time goes:
time: 390 us; the launch traced here: 389 us
  waiting for transfers between devices  232 us (59%)
  local copies, waits for them, and re-layouts  61.2 us (16%)
  matrix products  29.2 us (7%)
  starting transfers between devices  26.8 us (7%)
  other arithmetic  24.3 us (6%)
  between operations  14.4 us (4%)
    psum x1, waiting for transfers between devices, broadcast(): return lax.psum(jnp.where(mine, array, jnp.zeros_like(array)), axis)  104 us
    psum x1, waiting for transfers between devices, body(): global_total = lax.psum(pool_grads[edge_base:], 'ctx')  68.8 us
    all_to_all x1, waiting for transfers between devices, body(): lax.all_to_all(outgoing_grads, 'ctx', split_axis=0, concat_axis=0, tiled=...  39.2 us
    unnamed x24, local copies, waits for them, and re-layouts  9.57 us
    all_to_all x1, waiting for transfers between devices, body(): lax.all_to_all(queries, 'head', split_axis=1, concat_axis=0, tiled=True)  8.87 us
  transfers between devices with their start and end apart: 8, of which 6 were waited for; matrix products, arithmetic and copies ran while one was open for 6% of the time, Pallas kernels for 0%

commit v1 on v0

--- a/solution.py
+++ b/solution.py
@@ -148,7 +148,7 @@
     local_grads = local_grads + jnp.einsum(
         "dmq,dmtc->qtc", send_table, returned.astype(jnp.float32), precision=lax.Precision.HIGHEST
     )
-    global_total = lax.psum(pool_grads[edge_base:], "ctx")
+    global_total = jnp.sum(lax.all_gather(pool_grads[edge_base:], "ctx"), axis=0)
     local_grads = local_grads.at[:G].add(
         jnp.where(myself == 0, global_total, jnp.zeros_like(global_total))
     )

time: 390 us -> 349 us (0.89)
  the two profiles are of different devices: /device:TPU:0 before, /device:TPU:13 now
where the time goes in v1:
time: 349 us; the launch traced here: 348 us
  waiting for transfers between devices  184 us (53%)
  local copies, waits for them, and re-layouts  62.4 us (18%)
  starting transfers between devices  32.2 us (9%)
  matrix products  29.2 us (8%)
  other arithmetic  26 us (7%)
  between operations  14.4 us (4%)
    psum x1, waiting for transfers between devices, broadcast(): return lax.psum(jnp.where(mine, array, jnp.zeros_like(array)), axis)  102 us
    all_to_all x1, waiting for transfers between devices, body(): lax.all_to_all(outgoing_grads, 'ctx', split_axis=0, concat_axis=0, tiled=...  65.6 us
    unnamed x24, local copies, waits for them, and re-layouts  9.57 us
    all_to_all x1, starting transfers between devices, body(): lax.all_to_all(outgoing, 'ctx', split_axis=0, concat_axis=0, tiled=True)  9.55 us
    all_to_all x1, starting transfers between devices, body(): lax.all_to_all(outgoing_grads, 'ctx', split_axis=0, concat_axis=0, tiled=...  8.4 us
    all_to_all x1, waiting for transfers between devices, body(): lax.all_to_all(queries, 'head', split_axis=1, concat_axis=0, tiled=True)  7.35 us
  transfers between devices with their start and end apart: 8, of which 5 were waited for; matrix products, arithmetic and copies ran while one was open for 9% of the time, Pallas kernels for 0%

profile of v1, /device:TPU:13, one launch (start us, length us, event | category | flops | bytes accessed | tf_op | source)
XLA Modules:
  0.0 348.1 jit_solution(5090156928285502026)
XLA Ops:
  7.2 1.8 copy.205
  9.0 3.4 all-to-all-start.2
  13.8 2.1 copy.286
  18.2 3.4 all-to-all-start.1
  21.7 3.6 %all-to-all-done.1 = bf16[384,2,128]{0,2,1:T(8,128)(2,1)S(1)} async-done(((bf16[384,2,128]{0,2,1:T(8,128)(2,1)}), bf16[384,2,128]{0,2,1:T(8,128)(2,1)S(1)}, u32[]{:S(2)}, u32[]{:S(2)}) %all-to-all-start.1) | async-done | bytes 196640 | tf_op jit(solution)/shard_map/all_to_all | solution.py:57
  25.3 3.5 %all-to-all-start = ((bf16[384,2,512]{2,0,1:T(8,128)(2,1)}), bf16[384,2,512]{2,0,1:T(8,128)(2,1)S(1)}, u32[]{:S(2)}, u32[]{:S(2)}) async-start(bf16[384,2,512]{2,0,1:T(8,128)(2,1)} %bitcast.128), calls=%async_computation | async-start | bytes 1572864 | tf_op jit(solution)/shard_map/all_to_all | solution.py:56
  30.5 7.3 %all-to-all-done = bf16[384,2,512]{2,0,1:T(8,128)(2,1)S(1)} async-done(((bf16[384,2,512]{2,0,1:T(8,128)(2,1)}), bf16[384,2,512]{2,0,1:T(8,128)(2,1)S(1)}, u32[]{:S(2)}, u32[]{:S(2)}) %all-to-all-start) | async-done | bytes 786464 | tf_op jit(solution)/shard_map/all_to_all | solution.py:56
  37.8 3.5 %all-to-all-start.4 = ((bf16[384,2,512]{2,0,1:T(8,128)(2,1)}), bf16[384,2,512]{2,0,1:T(8,128)(2,1)S(1)}, u32[]{:S(2)}, u32[]{:S(2)}) async-start(bf16[384,2,512]{2,0,1:T(8,128)(2,1)} %bitcast.127), calls=%async_computation.4 | async-start | bytes 1572864 | tf_op jit(solution)/shard_map/all_to_all | solution.py:59
  42.4 2.1 copy.215
  44.5 4.9 %all-to-all-done.4 = bf16[384,2,512]{2,0,1:T(8,128)(2,1)S(1)} async-done(((bf16[384,2,512]{2,0,1:T(8,128)(2,1)}), bf16[384,2,512]{2,0,1:T(8,128)(2,1)S(1)}, u32[]{:S(2)}, u32[]{:S(2)}) %all-to-all-start.4) | async-done | bytes 786464 | tf_op jit(solution)/shard_map/all_to_all | solution.py:59
  50.4 9.5 %all-to-all-start.3 = ((bf16[16,2,128,256]{3,2,1,0:T(8,128)(2,1)}), bf16[16,2,128,256]{3,2,1,0:T(8,128)(2,1)S(1)}, u32[]{:S(2)}, u32[]{:S(2)}) async-start(bf16[16,2,128,256]{3,2,1,0:T(8,128)(2,1)} %copy.215), calls=%async_computation.3 | async-start | bytes 4194304 | tf_op jit(solution)/shard_map/all_to_all | solution.py:102
  61.9 1.5 fusion.29
  64.5 1.0 reshape.535
  65.6 1.7 reshape.537
  67.3 102.1 %all-reduce.2.cloned.1.call-done = bf16[2,128,256]{2,1,0:T(8,128)(2,1)} async-done(((bf16[2,128,256]{2,1,0:T(8,128)(2,1)}), bf16[2,128,256]{2,1,0:T(8,128)(2,1)}) %all-reduce.2.cloned.1.call-update) | async-done | bytes 131088 | tf_op jit(solution)/shard_map/psum | solution.py:18
  169.4 1.4 copy-done.2
  170.8 2.0 pad_maximum_fusion
  172.8 2.6 gather_fusion
  175.4 49.3 %while.13 = (s32[]{:T(128)}, bf16[6,128,4,128]{3,2,1,0:T(4,128)(2,1)}, f32[6,8,128,256]{2,3,1,0:T(8,128)}, pred[6,8]{1,0:T(8,128)(4,1)S(1)}, bf16[6,128,4,128]{3...) while((s32[]{:T(128)}, ...), condition=%wide.region_6.7_spmd, body=%wide.region_2.6_spmd.sunk | while | flops 814414336 | bytes 22569096 | solution.py:133
  175.4 1.1 dynamic-slice_bitcast_fusion.4
  182.5 1.1 fusion.107
  183.6 1.1 dynamic-slice_bitcast_fusion.4
  184.8 1.0 constant_dynamic-slice_fusion.5
  190.7 1.1 fusion.107
  191.8 1.1 dynamic-slice_bitcast_fusion.4
  193.0 1.0 constant_dynamic-slice_fusion.5
  198.9 1.1 fusion.107
  200.0 1.1 dynamic-slice_bitcast_fusion.4
  201.2 1.0 constant_dynamic-slice_fusion.5
  207.2 1.1 fusion.107
  208.2 1.1 dynamic-slice_bitcast_fusion.4
  215.4 1.1 fusion.107
  216.4 1.1 dynamic-slice_bitcast_fusion.4
  223.6 1.1 fusion.107
  224.7 3.4 convert_element_type.57
  228.1 1.1 copy-done
  229.3 3.9 %convert_select_fusion = f32[6,8,128,256]{2,3,1,0:T(8,128)} fusion(f32[6,8,128,256]{2,3,1,0:T(8,128)S(1)} %copy-done, bf16[6,8,128,256]{2,3,1,0:T(8,128)(2,1)S(1)} %convert_element_type.57, pred[6,8]{1,0:T(8,128)(4,1)S(1)} %compare_and_fusion.2), kind=kLoop, calls=%fused_computation.35 | loop fusion | flops 3145728 | bytes 15728688 | tf_op jit(solution)/shard_map/jit(_where)/select_n | solution.py:137
  233.1 6.7 %copy.226 = f32[6,8,128,256]{3,1,0,2:T(8,128)} copy(f32[6,8,128,256]{2,3,1,0:T(8,128)} %convert_select_fusion) | data formatting | bytes 12582912 | tf_op jit(solution)/shard_map/jit(_where)/select_n | solution.py:137
  239.8 5.0 %convolution_bitcast_fusion.2 = f32[40,128,256]{2,0,1:T(8,128)S(1)} fusion(f32[6,8,128,256]{3,1,0,2:T(8,128)} %copy.226, s32[6,8]{1,0:T(8,128)S(1)} %concatenate.68), kind=kOutput, calls=%fused_computation.38 | convolution fusion | flops 754976640 | bytes 11534528 | tf_op jit(solution)/shard_map/jnp,jntc->ptc/dot_general | solution.py:142
  244.9 2.3 copy-done.1
  248.0 4.5 %slice.74 = bf16[32,128,256]{2,0,1:T(8,128)(2,1)} slice(f32[40,128,256]{2,0,1:T(8,128)} %copy-done.1), slice={[6:38], [0:128], [0:256]} | slice | bytes 4194304 | tf_op jit(solution)/shard_map/slice | solution.py:145
  252.5 2.7 convert_element_type.59
  255.2 3.3 copy.227
  258.6 8.4 %all-to-all-start.5 = ((bf16[16,2,128,256]{3,1,2,0:T(2,128)(2,1)}), bf16[16,2,128,256]{3,1,2,0:T(2,128)(2,1)S(1)}, u32[]{:S(2)}, u32[]{:S(2)}) async-start(bf16[16,2,128,256]{3,1,2,0:T(2,128)(2,1)} %copy.227), calls=%async_computation.5 | async-start | bytes 4194304 | tf_op jit(solution)/shard_map/all_to_all | solution.py:147
  267.0 1.0 copy.284
  268.0 65.6 %all-to-all-done.5 = bf16[16,2,128,256]{3,1,2,0:T(2,128)(2,1)S(1)} async-done(((bf16[16,2,128,256]{3,1,2,0:T(2,128)(2,1)}), bf16[16,2,128,256]{3,1,2,0:T(2,128)(2,1)S(1)}, u32[]{:S(2)}, u32[]{:S(2)}) %all-to-all-start.5) | async-done | bytes 2097184 | tf_op jit(solution)/shard_map/all_to_all | solution.py:147
  333.6 3.2 fusion.24
  336.9 2.5 reduce_sum.37
  (159 shorter events, 46.0 us)
Async XLA Ops:
  7.2 8.8 %copy-start.8 = (bf16[384,256]{1,0:T(8,128)(2,1)S(1)}, bf16[384,256]{1,0:T(8,128)(2,1)}, u32[]{:S(2)}) copy-start(bf16[384,256]{1,0:T(8,128)(2,1)} %param.11) | copy-start | bytes 589828
  9.0 9.2 %all-to-all-start.2 = ((bf16[384,2,128]{0,2,1:T(8,128)(2,1)}), bf16[384,2,128]{0,2,1:T(8,128)(2,1)S(1)}, u32[]{:S(2)}, u32[]{:S(2)}) async-start(bf16[384,2,128]{0,2,1:T(8,128)(2,1)} %bitcast.24), calls=%async_computation.2 | async-start | bytes 393216 | tf_op jit(solution)/shard_map/all_to_all | solution.py:58
  13.8 15.2 %copy-start.6 = (bf16[384,1024]{1,0:T(8,128)(2,1)S(1)}, bf16[384,1024]{1,0:T(8,128)(2,1)}, u32[]{:S(2)}) copy-start(bf16[384,1024]{1,0:T(8,128)(2,1)} %param.13) | copy-start | bytes 2359300
  18.2 7.1 %all-to-all-start.1 = ((bf16[384,2,128]{0,2,1:T(8,128)(2,1)}), bf16[384,2,128]{0,2,1:T(8,128)(2,1)S(1)}, u32[]{:S(2)}, u32[]{:S(2)}) async-start(bf16[384,2,128]{0,2,1:T(8,128)(2,1)} %bitcast.21), calls=%async_computation.1 | async-start | bytes 393216 | tf_op jit(solution)/shard_map/all_to_all | solution.py:57
  25.3 12.5 %all-to-all-start = ((bf16[384,2,512]{2,0,1:T(8,128)(2,1)}), bf16[384,2,512]{2,0,1:T(8,128)(2,1)S(1)}, u32[]{:S(2)}, u32[]{:S(2)}) async-start(bf16[384,2,512]{2,0,1:T(8,128)(2,1)} %bitcast.128), calls=%async_computation | async-start | bytes 1572864 | tf_op jit(solution)/shard_map/all_to_all | solution.py:56
  30.1 12.3 %copy-start.4 = (bf16[2,384,128]{2,1,0:T(8,128)(2,1)}, bf16[2,384,128]{2,1,0:T(8,128)(2,1)S(1)}, u32[]{:S(2)}) copy-start(bf16[2,384,128]{2,1,0:T(8,128)(2,1)S(1)} %copy.206) | copy-start | bytes 589828
  30.3 7.5 %copy-start.5 = (bf16[2,384,128]{2,1,0:T(8,128)(2,1)}, bf16[2,384,128]{2,1,0:T(8,128)(2,1)S(1)}, u32[]{:S(2)}) copy-start(bf16[2,384,128]{2,1,0:T(8,128)(2,1)S(1)} %copy.204) | copy-start | bytes 589828
  37.8 11.6 %all-to-all-start.4 = ((bf16[384,2,512]{2,0,1:T(8,128)(2,1)}), bf16[384,2,512]{2,0,1:T(8,128)(2,1)S(1)}, u32[]{:S(2)}, u32[]{:S(2)}) async-start(bf16[384,2,512]{2,0,1:T(8,128)(2,1)} %bitcast.127), calls=%async_computation.4 | async-start | bytes 1572864 | tf_op jit(solution)/shard_map/all_to_all | solution.py:59
  44.5 17.0 %copy-start.9 = (s32[96]{0:T(128)S(1)}, s32[96]{0:T(128)}, u32[]{:S(2)}) copy-start(s32[96]{0:T(128)} %param.15) | copy-start | bytes 1156
  49.4 1.0 copy-start.3
  50.4 119.0 %all-to-all-start.3 = ((bf16[16,2,128,256]{3,2,1,0:T(8,128)(2,1)}), bf16[16,2,128,256]{3,2,1,0:T(8,128)(2,1)S(1)}, u32[]{:S(2)}, u32[]{:S(2)}) async-start(bf16[16,2,128,256]{3,2,1,0:T(8,128)(2,1)} %copy.215), calls=%async_computation.3 | async-start | bytes 4194304 | tf_op jit(solution)/shard_map/all_to_all | solution.py:102
  59.9 109.4 %all-reduce.2.cloned.1.call-start = ((), (), s32[]{:S(2)}) async-start(), calls=%async_computation.6 | async-start | bytes 262144 | tf_op jit(solution)/shard_map/psum | solution.py:18
  63.4 273.4 %all-gather.3.cloned.1.call-start = ((), (), s32[]{:S(2)}) async-start(), calls=%async_computation.7 | async-start | bytes 4456448 | tf_op jit(solution)/shard_map/all_gather | solution.py:151
  169.4 1.4 copy-start.2
  224.7 4.6 %copy-start = (f32[6,8,128,256]{2,3,1,0:T(8,128)S(1)}, f32[6,8,128,256]{2,3,1,0:T(8,128)}, u32[]{:S(2)}) copy-start(f32[6,8,128,256]{2,3,1,0:T(8,128)} %get-tuple-element.54) | copy-start | bytes 18874372
  244.9 2.3 copy-start.1
  258.6 8.4 %copy-start.7 = (bf16[6,128,4,128]{3,2,1,0:T(4,128)(2,1)S(1)}, bf16[6,128,4,128]{3,2,1,0:T(4,128)(2,1)}, u32[]{:S(2)}) copy-start(bf16[6,128,4,128]{3,2,1,0:T(4,128)(2,1)} %get-tuple-element.53) | copy-start | bytes 2359300
  258.6 75.0 %all-to-all-start.5 = ((bf16[16,2,128,256]{3,1,2,0:T(2,128)(2,1)}), bf16[16,2,128,256]{3,1,2,0:T(2,128)(2,1)S(1)}, u32[]{:S(2)}, u32[]{:S(2)}) async-start(bf16[16,2,128,256]{3,1,2,0:T(2,128)(2,1)} %copy.227), calls=%async_computation.5 | async-start | bytes 4194304 | tf_op jit(solution)/shard_map/all_to_all | solution.py:147
Sparse Core Ops, SparseCore 0:
  64.2 105.1 all-reduce.1
  248.1 77.2 all-gather.2
